TPU v7x, 32 devices: a whole 2x2x4 slice. The times are simulated.
32 devices in a mesh: row: 8 (over y, x, core), col: 4 (over z).
Axes of the slice: x: 2, y: 2, z: 4, core: 2. Of those that a mesh axis runs over, the one named last changes fastest.
Arguments:
- final_amp: bfloat16 [8, 32, 128, 440], P('row', 'col'), may hold values from -0.19921875 to 0.19921875
- initial_amp: bfloat16 [4, 32, 128, 440], P('col', 'row'), may hold values from -0.19921875 to 0.19921875
- pair_final: int32 [8, 4, 128], P('row', 'col'), may hold values from 0 to 31
- pair_initial: int32 [8, 4, 128], P('row', 'col'), may hold values from 0 to 31
- map_final: int32 [8, 32, 440], P('row', 'col'), may hold values from 0 to 439, each once within a row
- map_initial: int32 [4, 32, 440], P('col', 'row'), may hold values from 0 to 439, each once within a row
- counts: int32 [8, 4], P('row', 'col'), may hold values from 16 to 128, as said below
Outputs:
- density: float32 [440, 440], replicated
Inputs may be any that keep to these rules, and one draw needn't show every extreme that they name: `counts`: slots at or past a cell's count are ignored. Exactly one cell of every draw has 128 live slots.
All inputs are finite; a program needn't handle non-finite values.
Results may differ from a plain program's by a relative error of at most 0.0003.
Values may be sent and summed in bfloat16 or wider, within the bound.
A program may use at most 64 MiB of HBM per device.

v0:
```python
import jax
import jax.numpy as jnp
from jax import lax
from jax.sharding import PartitionSpec as P

GROUP = 32


def permute_columns(blocks, orbital_map):
    return jnp.take(blocks, orbital_map, axis=1)


def shards(final_amp, initial_amp, pair_final, pair_initial, map_final, map_initial, counts):
    own_final = jax.vmap(permute_columns)(final_amp[0], map_final[0])[None]
    own_initial = jax.vmap(permute_columns)(initial_amp[0], map_initial[0])[None]
    row_seg = lax.all_gather(own_final, "col", axis=1, tiled=True)[0]
    column_seg = lax.all_gather(own_initial, "row", axis=1, tiled=True)[0]
    slots_final = pair_final[0, 0]
    slots_initial = pair_initial[0, 0]
    live_count = counts[0, 0]
    orbitals = final_amp.shape[3]
    group_size = GROUP

    def advance(index, summed):
        first_slot = index * group_size
        which_final = lax.dynamic_slice_in_dim(slots_final, first_slot, group_size)
        which_initial = lax.dynamic_slice_in_dim(slots_initial, first_slot, group_size)
        live_mask = first_slot + jnp.arange(group_size, dtype=jnp.int32) < live_count
        left = jnp.take(row_seg, which_final, axis=0)
        right = jnp.take(column_seg, which_initial, axis=0)
        left = jnp.where(live_mask[:, None, None], left, jnp.zeros_like(left))
        product = lax.dot_general(
            left.reshape(-1, orbitals),
            right.reshape(-1, orbitals),
            (((0,), (0,)), ((), ())),
            preferred_element_type=jnp.float32,
        )
        return summed + product

    turns = (live_count + group_size - 1) // group_size
    partial_density = lax.fori_loop(0, turns, advance, jnp.zeros((orbitals, orbitals), jnp.float32))
    band = lax.psum_scatter(partial_density, "col", scatter_dimension=0, tiled=True)
    band = lax.psum(band, "row")
    density = lax.all_gather(band, "col", axis=0, tiled=True)
    return density


def solution(mesh):
    placed = (
        P("row", "col", None, None),
        P("col", "row", None, None),
        P("row", "col", None),
        P("row", "col", None),
        P("row", "col", None),
        P("col", "row", None),
        P("row", "col"),
    )
    return jax.shard_map(shards, mesh=mesh, in_specs=placed, out_specs=P(), check_vma=False)
```

profile of v0, /device:TPU:0, one launch (start us, length us, event | category | flops | bytes accessed | tf_op | source)
XLA Modules:
  0.0 321.1 jit_solution(12124861493017973160)
XLA Ops:
  6.5 0.0 copy-start
  6.5 0.0 all-gather.4.cloned.1.call-start
  6.5 0.8 fusion.18
  7.3 0.7 compare_and_fusion.2
  8.1 0.1 reshape.110
  8.2 0.0 copy-done
  8.2 0.0 copy-start.2
  8.2 0.0 copy-start.1
  8.2 30.8 %gather_fusion.2 = bf16[3520,128]{1,0:T(8,128)(2,1)S(1)} fusion(bf16[8,128,440]{1,2,0:T(8,128)(2,1)S(1)} %bitcast.44, s32[3520]{0:T(1024)S(1)} %reshape.110), kind=kCustom, calls=%fused_computation.2 | custom fusion | bytes 1830400 | tf_op jit(solution)/shard_map/vmap(jit(_take))/gather | solution.py:10
  39.0 1.4 broadcast_select_fusion
  40.4 0.0 all-gather.4.cloned.1.call-update
  40.4 0.0 all-gather.6.cloned.1.call-start
  40.4 0.0 copy-done.2
  40.5 0.1 reshape.116
  40.5 0.0 copy-done.1
  40.5 15.7 %gather_fusion.3 = bf16[1760,128]{1,0:T(8,128)(2,1)S(1)} fusion(bf16[4,128,440]{1,2,0:T(8,128)(2,1)S(1)} %bitcast.45, s32[1760]{0:T(1024)S(1)} %reshape.116), kind=kCustom, calls=%fused_computation.3 | custom fusion | bytes 915200 | tf_op jit(solution)/shard_map/vmap(jit(_take))/gather | solution.py:10
  56.3 1.1 broadcast_select_fusion.1
  57.4 0.0 all-gather.6.cloned.1.call-update
  57.4 0.0 all-reduce.4.cloned.1.call-start
  58.2 56.1 %all-gather.4.cloned.1.call-done = bf16[1,32,128,440]{2,3,0,1:T(8,128)(2,1)} async-done(((bf16[1,8,128,440]{2,3,0,1:T(8,128)(2,1)}), bf16[1,32,128,440]{2,3,0,1:T(8,128)(2,1)}) %all-gather.4.cloned.1.call-update) | async-done | bytes 3604496 | tf_op jit(solution)/shard_map/all_gather | solution.py:16
  114.3 6.4 %copy.18 = bf16[32,128,440]{2,1,0:T(8,128)(2,1)} copy(bf16[32,128,440]{1,2,0:T(8,128)(2,1)} %bitcast.47) | data formatting | bytes 7208960 | tf_op jit(solution)/shard_map/while | solution.py:41
  120.7 28.2 %all-gather.6.cloned.1.call-done = bf16[1,32,128,440]{2,3,0,1:T(8,128)(2,1)} async-done(((bf16[1,4,128,440]{2,3,0,1:T(8,128)(2,1)}), bf16[1,32,128,440]{2,3,0,1:T(8,128)(2,1)}) %all-gather.6.cloned.1.call-update) | async-done | bytes 3604496 | tf_op jit(solution)/shard_map/all_gather | solution.py:17
  148.9 6.5 %copy.19 = bf16[32,128,440]{2,1,0:T(8,128)(2,1)} copy(bf16[32,128,440]{1,2,0:T(8,128)(2,1)} %bitcast.48) | data formatting | bytes 7208960 | tf_op jit(solution)/shard_map/while | solution.py:41
  155.3 0.1 broadcast_in_dim.43
  155.5 0.0 copy-start.5
  155.5 33.5 %while.10 = (s32[]{:T(128)}, f32[440,440]{1,0:T(8,128)S(1)}, s32[]{:T(128)}, s32[]{:T(128)}, s32[128]{0:T(128)S(1)}, /*index=5*/bf16[32,128,440]{2,1,0:T(8,128)(...) while((s32[]{:T(128)}, f32[440,440]{1,0:T(8,128)S(1)}, ...), condition=%wide.region_1.3_spmd, body=%wide.region_0.0_spmd.sunk | while | flops 1591574016 | bytes 23185264 | solution.py:41
  155.5 0.1 compare_and_fusion.5
  155.6 5.0 %gather_fusion = bf16[32,128,440]{2,1,0:T(8,128)(2,1)} fusion(bf16[32,128,440]{2,1,0:T(8,128)(2,1)} %get-tuple-element.169, s32[1024]{0:T(1024)S(1)} %pad_clamp_fusion.4), kind=kCustom, calls=%fused_computation.1.clone.clone.1 | custom fusion | bytes 7209088 | tf_op jit(solution)/shard_map/while/body/jit(_take)/gather | solution.py:30
  160.6 4.9 %gather_fusion.1 = bf16[32,128,440]{2,1,0:T(8,128)(2,1)} fusion(bf16[32,128,440]{2,1,0:T(8,128)(2,1)} %get-tuple-element.167, s32[1024]{0:T(1024)S(1)} %pad_clamp_fusion.5), kind=kCustom, calls=%fused_computation.clone.clone.1 | custom fusion | bytes 7209088 | tf_op jit(solution)/shard_map/while/body/jit(_take)/gather | solution.py:29
  165.5 0.7 add_compare_fusion.2
  166.1 6.1 %fusion.25 = f32[440,440]{1,0:T(8,128)S(1)} fusion(f32[440,440]{1,0:T(8,128)S(1)} %get-tuple-element.151, bf16[32,128,440]{2,1,0:T(8,128)(2,1)} %gather_fusion, pred[32]{0:T(512)(128)(4,1)S(1)} %get-tuple-element.135, bf16[32,128,440]{2,1,0:T(8,128)(2,1)} %gather_fusion.1, pred[32]{0:T(512)(128)(4,1)S(1)} %get-tuple-element.137, ...), kind=kOutput, calls=%fused_computation.13.clone.1 | convolution fusion | flops 1591571456 | bytes 8757856 | tf_op jit(solution)/shard_map/while/body/dot_general | solution.py:32
  172.2 0.1 compare_and_fusion.5
  172.3 5.0 %gather_fusion = bf16[32,128,440]{2,1,0:T(8,128)(2,1)} fusion(bf16[32,128,440]{2,1,0:T(8,128)(2,1)} %get-tuple-element.169, s32[1024]{0:T(1024)S(1)} %pad_clamp_fusion.4), kind=kCustom, calls=%fused_computation.1.clone.clone.1 | custom fusion | bytes 7209088 | tf_op jit(solution)/shard_map/while/body/jit(_take)/gather | solution.py:30
  177.3 4.9 %gather_fusion.1 = bf16[32,128,440]{2,1,0:T(8,128)(2,1)} fusion(bf16[32,128,440]{2,1,0:T(8,128)(2,1)} %get-tuple-element.167, s32[1024]{0:T(1024)S(1)} %pad_clamp_fusion.5), kind=kCustom, calls=%fused_computation.clone.clone.1 | custom fusion | bytes 7209088 | tf_op jit(solution)/shard_map/while/body/jit(_take)/gather | solution.py:29
  182.2 0.7 add_compare_fusion.2
  182.9 6.1 %fusion.25 = f32[440,440]{1,0:T(8,128)S(1)} fusion(f32[440,440]{1,0:T(8,128)S(1)} %get-tuple-element.151, bf16[32,128,440]{2,1,0:T(8,128)(2,1)} %gather_fusion, pred[32]{0:T(512)(128)(4,1)S(1)} %get-tuple-element.135, bf16[32,128,440]{2,1,0:T(8,128)(2,1)} %gather_fusion.1, pred[32]{0:T(512)(128)(4,1)S(1)} %get-tuple-element.137, ...), kind=kOutput, calls=%fused_computation.13.clone.1 | convolution fusion | flops 1591571456 | bytes 8757856 | tf_op jit(solution)/shard_map/while/body/dot_general | solution.py:32
  188.9 22.8 %fusion = f32[112,440]{1,0:T(8,128)S(1)} fusion(f32[440,440]{1,0:T(8,128)S(1)} %get-tuple-element.49), kind=kCustom, calls=%all-reduce-scatter | all-reduce-scatter fusion | flops 197121 | bytes 972032
  211.7 2.1 collective-permute-start
  213.9 0.6 dynamic-slice.4
  215.1 0.2 collective-permute-done
  215.3 0.2 concatenate.6
  215.6 0.7 constant_dynamic-slice_fusion
  216.3 0.0 all-reduce.4.cloned.1.call-update
  216.3 74.9 %all-reduce.4.cloned.1.call-done = f32[110,440]{1,0:T(8,128)} async-done(((f32[110,440]{1,0:T(8,128)}), f32[110,440]{1,0:T(8,128)}) %all-reduce.4.cloned.1.call-update) | async-done | bytes 193616 | tf_op jit(solution)/shard_map/psum | solution.py:43
  291.2 1.1 copy.20
  292.3 20.9 %all-gather = f32[4,110,440]{1,2,0:T(8,128)S(1)} all-gather(f32[1,110,440]{1,2,0:T(8,128)S(1)} %copy.20), channel_id=1, replica_groups=mesh['row'=8,'col'=4] {'col'}, dimensions={0}, use_global_device_ids=true | all-gather | bytes 968000 | tf_op jit(solution)/shard_map/all_gather | solution.py:44
  313.2 0.4 copy.21
  313.6 1.0 reshape.125
  (12 shorter events, 0.1 us)
Async XLA Ops:
  6.5 1.6 copy-start
  6.5 107.7 %all-gather.4.cloned.1.call-start = ((), (), s32[]{:S(2)}) async-start(), calls=%async_computation | async-start | bytes 4505600 | tf_op jit(solution)/shard_map/all_gather | solution.py:16
  8.2 32.3 %copy-start.2 = (s32[1,4,440]{2,1,0:T(4,128)S(1)}, s32[1,4,440]{2,1,0:T(4,128)}, u32[]{:S(2)}) copy-start(s32[1,4,440]{2,1,0:T(4,128)} %param.16) | copy-start | bytes 21124
  8.2 32.4 %copy-start.1 = (bf16[1,4,128,440]{2,3,1,0:T(8,128)(2,1)S(1)}, bf16[1,4,128,440]{2,3,1,0:T(8,128)(2,1)}, u32[]{:S(2)}) copy-start(bf16[1,4,128,440]{2,3,1,0:T(8,128)(2,1)} %param.12) | copy-start | bytes 1351684
  40.4 108.5 %all-gather.6.cloned.1.call-start = ((), (), s32[]{:S(2)}) async-start(), calls=%async_computation.1 | async-start | bytes 4055040 | tf_op jit(solution)/shard_map/all_gather | solution.py:17
  57.4 233.8 %all-reduce.4.cloned.1.call-start = ((), (), s32[]{:S(2)}) async-start(), calls=%async_computation.2 | async-start | bytes 458752 | tf_op jit(solution)/shard_map/psum | solution.py:43
  148.9 6.6 %copy-start.3 = (s32[1,1,128]{2,1,0:T(1,128)S(1)}, s32[1,1,128]{2,1,0:T(1,128)}, u32[]{:S(2)}) copy-start(s32[1,1,128]{2,1,0:T(1,128)} %param.13) | copy-start | bytes 1540
  148.9 6.6 %copy-start.4 = (s32[1,1,128]{2,1,0:T(1,128)S(1)}, s32[1,1,128]{2,1,0:T(1,128)}, u32[]{:S(2)}) copy-start(s32[1,1,128]{2,1,0:T(1,128)} %param.14) | copy-start | bytes 1540
  155.5 58.4 %copy-start.5 = (u32[32]{0:T(128)S(1)}, u32[32]{0:T(128)}, u32[]{:S(2)}) copy-start(u32[32]{0:T(128)} %constant.104) | copy-start | bytes 388
  211.7 3.6 %collective-permute-start = (f32[6,440]{1,0:T(8,128)S(1)}, f32[6,440]{1,0:T(8,128)S(1)}, u32[]{:S(2)}, u32[]{:S(2)}) collective-permute-start(f32[6,440]{1,0:T(8,128)S(1)} %slice.8), channel_id=1, source_target_pairs={{0,1},{1,2},{2,3},{4,5},{5,6},{6,7},{8,9},{9,10},{10,11},{12,13},{... | collective-permute-start | bytes 31688
Sparse Core Ops, SparseCore 0:
  40.5 73.7 all-gather.3
  116.2 32.6 all-gather.5
  216.4 74.7 all-reduce.3
where the time goes:
time: 322 us; the launch traced here: 321 us
  waiting for transfers between devices  159 us (49%)
  local copies, waits for them, and re-layouts  83.4 us (26%)
  blocking collectives  43.7 us (14%)
  between operations  14.6 us (5%)
  matrix products  12.1 us (4%)
  other arithmetic  5.57 us (2%)
    psum x1, waiting for transfers between devices, shards(): band = lax.psum(band, 'row')  74.9 us
    all_gather x1, waiting for transfers between devices, shards(): row_seg = lax.all_gather(own_final, 'col', axis=1, tiled=True)[0]  56.1 us
    gather x4, local copies, waits for them, and re-layouts, permute_columns(): return jnp.take(blocks, orbital_map, axis=1)  46.6 us
    all_gather x1, waiting for transfers between devices, shards(): column_seg = lax.all_gather(own_initial, 'row', axis=1, tiled=True)[0]  28.2 us
    unnamed x1, blocking collectives  22.8 us
    all_gather x1, blocking collectives, shards(): density = lax.all_gather(band, 'col', axis=0, tiled=True)  20.9 us
    while x2, local copies, waits for them, and re-layouts, shards(): lax.fori_loop(0, turns, advance, jnp.zeros((orbitals, orbitals), jnp.floa...  12.9 us
    dot_general x2, matrix products, advance(): lax.dot_general(left.reshape(-1, orbitals), right.reshape(-1, orbitals),...  12.1 us
  transfers between devices with their start and end apart: 4, of which 4 were waited for; matrix products, arithmetic and copies ran while one was open for 7% of the time, Pallas kernels for 0%

commit v1 on v0

--- a/solution.py
+++ b/solution.py
@@ -4,6 +4,23 @@
 from jax.sharding import PartitionSpec as P
 
 GROUP = 32
+
+
+def joined_along(blocks, dim):
+    shape = list(blocks.shape[1:])
+    shape[dim] *= blocks.shape[0]
+    return jnp.moveaxis(blocks, 0, dim).reshape(shape)
+
+
+def gather_around(x, axis, dim):
+    peers = lax.axis_size(axis)
+    upward = [(i, (i + 1) % peers) for i in range(peers)]
+    blocks = [x]
+    while len(blocks) < peers:
+        blocks.append(lax.ppermute(blocks[-1], axis, upward))
+    mine = lax.axis_index(axis)
+    blocks = jnp.stack(blocks)[(mine - jnp.arange(peers)) % peers]
+    return joined_along(blocks, dim)
 
 
 def permute_columns(blocks, orbital_map):
@@ -13,7 +30,7 @@
 def shards(final_amp, initial_amp, pair_final, pair_initial, map_final, map_initial, counts):
     own_final = jax.vmap(permute_columns)(final_amp[0], map_final[0])[None]
     own_initial = jax.vmap(permute_columns)(initial_amp[0], map_initial[0])[None]
-    row_seg = lax.all_gather(own_final, "col", axis=1, tiled=True)[0]
+    row_seg = gather_around(own_final, "col", 1)[0]
     column_seg = lax.all_gather(own_initial, "row", axis=1, tiled=True)[0]
     slots_final = pair_final[0, 0]
     slots_initial = pair_initial[0, 0]

time: 322 us -> 308 us (0.957)
  waiting for transfers between devices: 159 us -> 137 us
  local copies, waits for them, and re-layouts: 83.4 us -> 89.1 us
  blocking collectives: 43.7 us -> 39.4 us
  starting transfers between devices: 2.22 us -> 6.2 us
    ppermute x0 -> x3, waiting for transfers between devices: none -> 66.1 us  [gather_around(): blocks.append(lax.ppermute(blocks[-1], axis, upward))]
    all_gather x1 -> x0, waiting for transfers between devices: 56.1 us -> none  [shards(): row_seg = lax.all_gather(own_final, 'col', axis=1, tiled=True)[0]]
    all_gather x1, waiting for transfers between devices: 28.2 us -> 0.01 us  [shards(): column_seg = lax.all_gather(own_initial, 'row', axis=1, tiled=True)[0]]
    gather x0 -> x2, local copies, waits for them, and re-layouts: none -> 11 us  [gather_around(): blocks = jnp.stack(blocks)[(mine - jnp.arange(peers)) % peers]]
    while x2 -> x1, local copies, waits for them, and re-layouts: 12.9 us -> 6.46 us  [shards(): lax.fori_loop(0, turns, advance, jnp.zeros((orbitals, orbitals), jnp.floa...]
    psum x1, waiting for transfers between devices: 74.9 us -> 70.4 us  [shards(): band = lax.psum(band, 'row')]
    unnamed x1, blocking collectives: 22.8 us -> 18.5 us
  transfers between devices with their start and end apart: 4 -> 6, of which waited for: 4 -> 5; matrix products, arithmetic and copies ran while one was open for 7% -> 15% of each run, Pallas kernels for 0% -> 0%
where the time goes in v1:
time: 308 us; the launch traced here: 307 us
  waiting for transfers between devices  137 us (44%)
  local copies, waits for them, and re-layouts  89.1 us (29%)
  blocking collectives  39.4 us (13%)
  between operations  14.9 us (5%)
  matrix products  12.1 us (4%)
  other arithmetic  8.56 us (3%)
  starting transfers between devices  6.2 us (2%)
    psum x1, waiting for transfers between devices, shards(): band = lax.psum(band, 'row')  70.4 us
    ppermute x3, waiting for transfers between devices, gather_around(): blocks.append(lax.ppermute(blocks[-1], axis, upward))  66.1 us
    gather x4, local copies, waits for them, and re-layouts, permute_columns(): return jnp.take(blocks, orbital_map, axis=1)  47.7 us
    all_gather x1, blocking collectives, shards(): density = lax.all_gather(band, 'col', axis=0, tiled=True)  20.9 us
    unnamed x1, blocking collectives  18.5 us
    dot_general x2, matrix products, advance(): lax.dot_general(left.reshape(-1, orbitals), right.reshape(-1, orbitals),...  12.1 us
    gather x2, local copies, waits for them, and re-layouts, gather_around(): blocks = jnp.stack(blocks)[(mine - jnp.arange(peers)) % peers]  11 us
    gather x2, local copies, waits for them, and re-layouts, advance(): right = jnp.take(column_seg, which_initial, axis=0)  9.93 us
  transfers between devices with their start and end apart: 6, of which 5 were waited for; matrix products, arithmetic and copies ran while one was open for 15% of the time, Pallas kernels for 0%

profile of v1, /device:TPU:0, one launch (start us, length us, event | category | flops | bytes accessed | tf_op | source)
XLA Modules:
  0.0 307.1 jit_solution(8209272381759934323)
XLA Ops:
  6.5 0.8 fusion.21
  7.3 0.7 compare_and_fusion.3
  8.0 0.1 reshape.182
  8.1 16.7 %gather_fusion.4 = bf16[1760,128]{1,0:T(8,128)(2,1)S(1)} fusion(bf16[4,128,440]{1,2,0:T(8,128)(2,1)} %bitcast.55, s32[1760]{0:T(1024)S(1)} %reshape.182), kind=kCustom, calls=%fused_computation.4 | custom fusion | bytes 915200 | tf_op jit(solution)/shard_map/vmap(jit(_take))/gather | solution.py:27
  24.9 1.1 broadcast_select_fusion.2
  25.9 0.0 all-gather.3.cloned.1.call-update
  26.0 0.0 all-reduce.4.cloned.1.call-start
  26.0 0.0 copy-done.1
  26.0 0.1 reshape.176
  26.1 0.0 copy-done
  26.1 30.8 %gather_fusion.3 = bf16[3520,128]{1,0:T(8,128)(2,1)S(1)} fusion(bf16[8,128,440]{1,2,0:T(8,128)(2,1)S(1)} %bitcast.53, s32[3520]{0:T(1024)S(1)} %reshape.176), kind=kCustom, calls=%fused_computation.3 | custom fusion | bytes 1830400 | tf_op jit(solution)/shard_map/vmap(jit(_take))/gather | solution.py:27
  56.9 0.7 broadcast_select_fusion
  57.6 3.1 %collective-permute-start = (bf16[1,8,128,440]{2,3,1,0:T(8,128)(2,1)S(1)}, bf16[1,8,128,440]{2,3,1,0:T(8,128)(2,1)S(1)}, u32[]{:S(2)}, u32[]{:S(2)}) collective-permute-start(bf16[1,8,128,440]{2,3,1,0:T(8,128)(2,1)S(1)} %broadcast_select_fusion), channel_id=1, source_target_pairs={{0,1},{1,2},{2,3},{3,0},{4,5},{5,6},{6,7},{7,4},{8,9},{9,10},{10,1... | collective-permute-start | bytes 2703368 | tf_op jit(solution)/shard_map/ppermute | solution.py:20
  60.7 22.0 %collective-permute-done = bf16[1,8,128,440]{2,3,1,0:T(8,128)(2,1)S(1)} collective-permute-done((bf16[1,8,128,440]{2,3,1,0:T(8,128)(2,1)S(1)}, bf16[1,8,128,440]{2,3,1,0:T(8,128)(2,1)S(1)}, u32[]{:S(2)}, u32[]{:S(2)}) %collective-permute-start) | collective-permute-done | bytes 901152 | tf_op jit(solution)/shard_map/ppermute | solution.py:20
  82.7 0.0 collective-permute-start.1
  82.7 23.1 %collective-permute-done.1 = bf16[1,8,128,440]{2,3,1,0:T(8,128)(2,1)} collective-permute-done((bf16[1,8,128,440]{2,3,1,0:T(8,128)(2,1)S(1)}, bf16[1,8,128,440]{2,3,1,0:T(8,128)(2,1)}, u32[]{:S(2)}, u32[]{:S(2)}) %collective-permute-start.1) | collective-permute-done | bytes 901152 | tf_op jit(solution)/shard_map/ppermute | solution.py:20
  105.8 0.0 collective-permute-start.2
  106.5 0.7 broadcast_select_fusion.1
  107.1 21.1 %collective-permute-done.2 = bf16[1,8,128,440]{2,3,1,0:T(8,128)(2,1)} collective-permute-done((bf16[1,8,128,440]{2,3,1,0:T(8,128)(2,1)}, bf16[1,8,128,440]{2,3,1,0:T(8,128)(2,1)}, u32[]{:S(2)}, u32[]{:S(2)}) %collective-permute-start.2) | collective-permute-done | bytes 901152 | tf_op jit(solution)/shard_map/ppermute | solution.py:20
  128.2 3.2 %maximum_bitcast_fusion = bf16[4,8,128,440]{2,3,1,0:T(8,128)(2,1)} fusion(bf16[1,1,8,128,440]{3,4,2,1,0:T(8,128)(2,1)} %bitcast.13, bf16[1,1,8,128,440]{3,4,2,1,0:T(8,128)(2,1)} %bitcast.12, bf16[1,1,8,128,440]{3,4,2,1,0:T(8,128)(2,1)S(1)} %bitcast.60, bf16[1,1,8,128,440]{3,4,2,1,0:T(8,128)(2,1)S(1)} %broadcast_select_fusion.1), kind=kLoop, calls=%fused_computation.24 | loop fusion | flops 5406720 | bytes 7208960 | tf_op jit(solution)/shard_map/stack | solution.py:22
  131.4 4.8 %gather_fusion.2 = bf16[4,8,128,440]{2,3,1,0:T(8,128)(2,1)} fusion(bf16[4,8,128,440]{2,3,1,0:T(8,128)(2,1)} %maximum_bitcast_fusion, s32[1024]{0:T(1024)S(1)} %pad_clamp_fusion.2), kind=kCustom, calls=%fused_computation.2 | custom fusion | bytes 7208976 | tf_op jit(solution)/shard_map/gather | solution.py:22
  136.2 6.2 %copy.18 = bf16[4,8,128,440]{3,2,1,0:T(8,128)(2,1)} copy(bf16[4,8,128,440]{2,3,1,0:T(8,128)(2,1)} %gather_fusion.2) | data formatting | bytes 7208960 | tf_op jit(solution)/shard_map/gather | solution.py:22
  142.4 6.5 %copy.19 = bf16[32,128,440]{2,1,0:T(8,128)(2,1)} copy(bf16[32,128,440]{1,2,0:T(8,128)(2,1)} %bitcast.58) | data formatting | bytes 7208960 | tf_op jit(solution)/shard_map/while | solution.py:58
  148.8 0.1 broadcast_in_dim.48
  149.0 0.0 copy-start.4
  149.0 33.5 %while.10 = (s32[]{:T(128)}, f32[440,440]{1,0:T(8,128)S(1)}, s32[]{:T(128)}, s32[]{:T(128)}, s32[128]{0:T(128)S(1)}, /*index=5*/bf16[32,128,440]{2,1,0:T(8,128)(...) while((s32[]{:T(128)}, f32[440,440]{1,0:T(8,128)S(1)}, ...), condition=%wide.region_1.3_spmd, body=%wide.region_0.0_spmd.sunk | while | flops 1591574016 | bytes 23185264 | solution.py:58
  149.0 0.1 compare_and_fusion.5
  149.1 4.9 %gather_fusion.1 = bf16[32,128,440]{2,1,0:T(8,128)(2,1)} fusion(bf16[32,128,440]{2,1,0:T(8,128)(2,1)} %get-tuple-element.167, s32[1024]{0:T(1024)S(1)} %pad_clamp_fusion.6), kind=kCustom, calls=%fused_computation.clone.clone.1 | custom fusion | bytes 7209088 | tf_op jit(solution)/shard_map/while/body/jit(_take)/gather | solution.py:46
  154.0 5.0 %gather_fusion = bf16[32,128,440]{2,1,0:T(8,128)(2,1)} fusion(bf16[32,128,440]{2,1,0:T(8,128)(2,1)} %get-tuple-element.169, s32[1024]{0:T(1024)S(1)} %pad_clamp_fusion.5), kind=kCustom, calls=%fused_computation.1.clone.clone.1 | custom fusion | bytes 7209088 | tf_op jit(solution)/shard_map/while/body/jit(_take)/gather | solution.py:47
  159.0 0.7 add_compare_fusion.2
  159.7 6.1 %fusion.27 = f32[440,440]{1,0:T(8,128)S(1)} fusion(f32[440,440]{1,0:T(8,128)S(1)} %get-tuple-element.151, bf16[32,128,440]{2,1,0:T(8,128)(2,1)} %gather_fusion, pred[32]{0:T(512)(128)(4,1)S(1)} %get-tuple-element.135, bf16[32,128,440]{2,1,0:T(8,128)(2,1)} %gather_fusion.1, pred[32]{0:T(512)(128)(4,1)S(1)} %get-tuple-element.137, ...), kind=kOutput, calls=%fused_computation.14.clone.1 | convolution fusion | flops 1591571456 | bytes 8757856 | tf_op jit(solution)/shard_map/while/body/dot_general | solution.py:49
  165.7 0.1 compare_and_fusion.5
  165.8 4.9 %gather_fusion.1 = bf16[32,128,440]{2,1,0:T(8,128)(2,1)} fusion(bf16[32,128,440]{2,1,0:T(8,128)(2,1)} %get-tuple-element.167, s32[1024]{0:T(1024)S(1)} %pad_clamp_fusion.6), kind=kCustom, calls=%fused_computation.clone.clone.1 | custom fusion | bytes 7209088 | tf_op jit(solution)/shard_map/while/body/jit(_take)/gather | solution.py:46
  170.8 5.0 %gather_fusion = bf16[32,128,440]{2,1,0:T(8,128)(2,1)} fusion(bf16[32,128,440]{2,1,0:T(8,128)(2,1)} %get-tuple-element.169, s32[1024]{0:T(1024)S(1)} %pad_clamp_fusion.5), kind=kCustom, calls=%fused_computation.1.clone.clone.1 | custom fusion | bytes 7209088 | tf_op jit(solution)/shard_map/while/body/jit(_take)/gather | solution.py:47
  175.7 0.7 add_compare_fusion.2
  176.4 6.1 %fusion.27 = f32[440,440]{1,0:T(8,128)S(1)} fusion(f32[440,440]{1,0:T(8,128)S(1)} %get-tuple-element.151, bf16[32,128,440]{2,1,0:T(8,128)(2,1)} %gather_fusion, pred[32]{0:T(512)(128)(4,1)S(1)} %get-tuple-element.135, bf16[32,128,440]{2,1,0:T(8,128)(2,1)} %gather_fusion.1, pred[32]{0:T(512)(128)(4,1)S(1)} %get-tuple-element.137, ...), kind=kOutput, calls=%fused_computation.14.clone.1 | convolution fusion | flops 1591571456 | bytes 8757856 | tf_op jit(solution)/shard_map/while/body/dot_general | solution.py:49
  182.5 18.5 %fusion = f32[112,440]{1,0:T(8,128)S(1)} fusion(f32[440,440]{1,0:T(8,128)S(1)} %get-tuple-element.49), kind=kCustom, calls=%all-reduce-scatter | all-reduce-scatter fusion | flops 197121 | bytes 972032
  201.0 3.0 collective-permute-start.3
  204.1 0.6 dynamic-slice.4
  205.3 0.2 collective-permute-done.3
  205.5 0.2 concatenate.6
  205.8 0.7 constant_dynamic-slice_fusion
  206.5 0.0 all-reduce.4.cloned.1.call-update
  206.5 70.4 %all-reduce.4.cloned.1.call-done = f32[110,440]{1,0:T(8,128)} async-done(((f32[110,440]{1,0:T(8,128)}), f32[110,440]{1,0:T(8,128)}) %all-reduce.4.cloned.1.call-update) | async-done | bytes 193616 | tf_op jit(solution)/shard_map/psum | solution.py:60
  276.9 1.1 copy.20
  278.0 20.9 %all-gather = f32[4,110,440]{1,2,0:T(8,128)S(1)} all-gather(f32[1,110,440]{1,2,0:T(8,128)S(1)} %copy.20), channel_id=1, replica_groups=mesh['row'=8,'col'=4] {'col'}, dimensions={0}, use_global_device_ids=true | all-gather | bytes 968000 | tf_op jit(solution)/shard_map/all_gather | solution.py:61
  298.9 0.4 copy.21
  299.3 1.0 reshape.192
  (18 shorter events, 0.1 us)
Async XLA Ops:
  6.5 19.6 %copy-start = (bf16[1,8,128,440]{2,3,1,0:T(8,128)(2,1)S(1)}, bf16[1,8,128,440]{2,3,1,0:T(8,128)(2,1)}, u32[]{:S(2)}) copy-start(bf16[1,8,128,440]{2,3,1,0:T(8,128)(2,1)} %param.11) | copy-start | bytes 2703364
  6.5 19.5 %copy-start.1 = (s32[1,8,440]{2,1,0:T(8,128)S(1)}, s32[1,8,440]{2,1,0:T(8,128)}, u32[]{:S(2)}) copy-start(s32[1,8,440]{2,1,0:T(8,128)} %param.15) | copy-start | bytes 42244
  6.5 135.8 %all-gather.3.cloned.1.call-start = ((), (), s32[]{:S(2)}) async-start(), calls=%async_computation | async-start | bytes 4055040 | tf_op jit(solution)/shard_map/all_gather | solution.py:34
  26.0 250.9 %all-reduce.4.cloned.1.call-start = ((), (), s32[]{:S(2)}) async-start(), calls=%async_computation.1 | async-start | bytes 458752 | tf_op jit(solution)/shard_map/psum | solution.py:60
  57.6 25.1 %collective-permute-start = (bf16[1,8,128,440]{2,3,1,0:T(8,128)(2,1)S(1)}, bf16[1,8,128,440]{2,3,1,0:T(8,128)(2,1)S(1)}, u32[]{:S(2)}, u32[]{:S(2)}) collective-permute-start(bf16[1,8,128,440]{2,3,1,0:T(8,128)(2,1)S(1)} %broadcast_select_fusion), channel_id=1, source_target_pairs={{0,1},{1,2},{2,3},{3,0},{4,5},{5,6},{6,7},{7,4},{8,9},{9,10},{10,1... | collective-permute-start | bytes 2703368 | tf_op jit(solution)/shard_map/ppermute | solution.py:20
  82.7 23.1 %collective-permute-start.1 = (bf16[1,8,128,440]{2,3,1,0:T(8,128)(2,1)S(1)}, bf16[1,8,128,440]{2,3,1,0:T(8,128)(2,1)}, u32[]{:S(2)}, u32[]{:S(2)}) collective-permute-start(bf16[1,8,128,440]{2,3,1,0:T(8,128)(2,1)S(1)} %collective-permute-done), channel_id=1, source_target_pairs={{0,1},{1,2},{2,3},{3,0},{4,5},{5,6},{6,7},{7,4},{8,9},{9,10},{10,1... | collective-permute-start | bytes 2703368 | tf_op jit(solution)/shard_map/ppermute | solution.py:20
  105.8 22.4 %collective-permute-start.2 = (bf16[1,8,128,440]{2,3,1,0:T(8,128)(2,1)}, bf16[1,8,128,440]{2,3,1,0:T(8,128)(2,1)}, u32[]{:S(2)}, u32[]{:S(2)}) collective-permute-start(bf16[1,8,128,440]{2,3,1,0:T(8,128)(2,1)} %collective-permute-done.1), channel_id=1, source_target_pairs={{0,1},{1,2},{2,3},{3,0},{4,5},{5,6},{6,7},{7,4},{8,9},{9,10},{10,1... | collective-permute-start | bytes 2703368 | tf_op jit(solution)/shard_map/ppermute | solution.py:20
  142.4 6.6 %copy-start.2 = (s32[1,1,128]{2,1,0:T(1,128)S(1)}, s32[1,1,128]{2,1,0:T(1,128)}, u32[]{:S(2)}) copy-start(s32[1,1,128]{2,1,0:T(1,128)} %param.13) | copy-start | bytes 1540
  142.4 6.6 %copy-start.3 = (s32[1,1,128]{2,1,0:T(1,128)S(1)}, s32[1,1,128]{2,1,0:T(1,128)}, u32[]{:S(2)}) copy-start(s32[1,1,128]{2,1,0:T(1,128)} %param.14) | copy-start | bytes 1540
  149.0 55.1 %copy-start.4 = (u32[32]{0:T(128)S(1)}, u32[32]{0:T(128)}, u32[]{:S(2)}) copy-start(u32[32]{0:T(128)} %constant.124) | copy-start | bytes 388
  201.0 4.5 %collective-permute-start.3 = (f32[6,440]{1,0:T(8,128)S(1)}, f32[6,440]{1,0:T(8,128)S(1)}, u32[]{:S(2)}, u32[]{:S(2)}) collective-permute-start(f32[6,440]{1,0:T(8,128)S(1)} %slice.10), channel_id=1, source_target_pairs={{0,1},{1,2},{2,3},{4,5},{5,6},{6,7},{8,9},{9,10},{10,11},{12,13},{... | collective-permute-start | bytes 31688
Sparse Core Ops, SparseCore 0:
  26.1 36.8 all-gather.2
  206.6 70.2 all-reduce.3
